TPU v7x, 128 devices: a whole 4x4x4 slice. The times are simulated.
128 devices in a mesh: row: 8 (over y, core), col: 16 (over z, x).
Axes of the slice: x: 4, y: 4, z: 4, core: 2. Of those that a mesh axis runs over, the one named last changes fastest.
Arguments:
- wavefunction: bfloat16 [32, 16, 256, 256], P('row', 'col'), may hold values from -6 to 6
- env_left: bfloat16 [16, 32, 2, 256, 256], P('col', 'row'), may hold values from -0.25 to 0.25
- left_src: int32 [16, 32, 2], P('col', 'row'), may hold values from 0 to 3
- two_site: bfloat16 [16, 16, 16], P('col'), may hold values from -1.5 to 1.5
- env_right: bfloat16 [16, 32, 256, 256], P('col', 'row'), may hold values from -0.09375 to 0.09375
- right_loc: int32 [32, 16], P('row', 'col'), may hold values from 0 to 3
- left_size: int32 [32], P('row'), may hold values from 128 to 256
- right_size: int32 [32], P('row'), may hold values from 128 to 256
Outputs:
- applied: bfloat16 [32, 16, 256, 256], P('row', 'col')
All inputs are finite; a program needn't handle non-finite values.
Results may differ from a plain program's by a relative error of at most 0.018.
Values may be sent and summed in bfloat16 or wider, within the bound.
No kernel may reach another device: no remote copies, remote signals or barrier semaphores. Data moves between devices by JAX's collectives and lax.ppermute only.
A program may use at most 128 MiB of HBM per device.

v0:
```python
import jax
import jax.numpy as jnp
from jax import lax
from jax.sharding import PartitionSpec as P


def per_device(
    wavefunction, env_left, left_src, two_site, env_right, right_loc, left_size, right_size
):
    whole, whole_loc = (
        lax.all_gather(wavefunction, "col", axis=1, tiled=True),
        lax.all_gather(right_loc, "col", axis=1, tiled=True),
    )
    local_tiles = wavefunction.shape[0]
    tile_width = wavefunction.shape[3]
    mixed_rows = []
    for position in range(local_tiles):
        blocks = whole[left_src[0, position]]
        left_part = jnp.einsum(
            "kxy,ksyz->sxz", env_left[0, position], blocks, preferred_element_type=jnp.float32
        ).astype(jnp.bfloat16)
        mixed_rows.append(
            jnp.einsum(
                "ts,sxz->txz", two_site[0], left_part, preferred_element_type=jnp.float32
            ).astype(jnp.bfloat16)
        )
    mixed = jnp.stack(mixed_rows)
    col_iota = lax.broadcasted_iota(jnp.int32, (1, 1, tile_width), 2)
    received, recv_loc = (
        lax.all_to_all(mixed, "row", split_axis=1, concat_axis=0, tiled=True),
        lax.all_to_all(whole_loc, "row", split_axis=1, concat_axis=0, tiled=True),
    )
    pieces = []
    for column in range(received.shape[1]):
        chosen = env_right[0][recv_loc[:, column]]
        product = jnp.einsum(
            "axy,azy->axz", received[:, column], chosen, preferred_element_type=jnp.float32
        )
        col_limit = right_size[recv_loc[:, column]]
        inside = col_iota < col_limit[:, None, None]
        pieces.append(jnp.where(inside, product, 0.0).astype(jnp.bfloat16))
    term = lax.all_to_all(jnp.stack(pieces, axis=1), "row", split_axis=0, concat_axis=1, tiled=True)
    summed = lax.psum_scatter(
        term.astype(jnp.float32).astype(jnp.bfloat16), "col", scatter_dimension=1, tiled=True
    ).astype(jnp.float32)
    row_iota = lax.broadcasted_iota(jnp.int32, summed.shape, 2)
    inside_rows = row_iota < left_size[:, None, None, None]
    return jnp.where(inside_rows, summed, 0.0).astype(jnp.bfloat16)


def solution(mesh):
    placed = (
        P("row", "col", None, None),
        P("col", "row", None, None, None),
        P("col", "row", None),
        P("col", None, None),
        P("col", "row", None, None),
        P("row", "col"),
        P("row"),
        P("row"),
    )
    return jax.shard_map(
        per_device,
        mesh=mesh,
        in_specs=placed,
        out_specs=P("row", "col", None, None),
        check_vma=False,
    )
```

profile of v0, /device:TPU:1, one launch (start us, length us, event | category | flops | bytes accessed | tf_op | source)
XLA Modules:
  0.0 596.2 jit_solution(1501007717909477833)
XLA Ops:
  6.5 0.0 copy-start
  6.5 0.7 all-gather.3.cloned.1.call-update
  7.3 18.3 %all-gather = s32[16,1,4]{2,1,0:T(1,128)S(1)} all-gather(s32[1,1,4]{2,1,0:T(1,128)} %bitcast.158), channel_id=1, replica_groups=mesh['row'=8,'col'=16] {'col'}, dimensions={0}, use_global_device_ids=true | all-gather | bytes 272 | tf_op jit(solution)/shard_map/all_gather | solution.py:12
  25.5 0.1 copy.30
  25.6 0.7 copy.31
  26.3 9.6 %all-to-all-start = ((s32[4,8,2]{0,2,1:T(2,128)}), s32[4,8,2]{0,2,1:T(2,128)S(1)}, u32[]{:S(2)}, u32[]{:S(2)}) async-start(s32[4,8,2]{0,2,1:T(2,128)} %bitcast.3), calls=%async_computation | async-start | bytes 16384 | tf_op jit(solution)/shard_map/all_to_all | solution.py:31
  35.9 1.0 slice_reduce_fusion.3
  37.0 46.7 %all-gather.3.cloned.1.call-done = bf16[4,16,256,256]{3,2,1,0:T(8,128)(2,1)} async-done(((bf16[4,1,256,256]{3,2,1,0:T(8,128)(2,1)}), bf16[4,16,256,256]{3,2,1,0:T(8,128)(2,1)}) %all-gather.3.cloned.1.call-update) | async-done | bytes 8388624 | tf_op jit(solution)/shard_map/all_gather | solution.py:11
  83.7 6.0 fusion.62
  89.6 2.9 gather_fusion.6
  92.5 4.2 gather_fusion.7
  96.7 4.2 gather_fusion.4
  100.9 4.2 gather_fusion.5
  105.1 4.2 gather_fusion.2
  109.3 4.2 gather_fusion.3
  113.6 4.2 gather_fusion.8
  117.8 4.2 gather_fusion.9
  122.0 2.4 copy.39
  124.4 4.1 copy.40
  128.5 4.2 fusion.34
  132.7 3.3 copy.41
  136.0 4.0 copy.36
  140.0 4.0 copy.37
  144.0 4.9 fusion.31
  148.8 4.6 copy.38
  153.4 2.1 convert_bitcast_fusion.1
  155.5 2.0 convert_bitcast_fusion.2
  157.5 3.9 copy.33
  161.5 2.4 copy.34
  163.8 4.9 fusion.28
  168.7 3.3 copy.35
  172.1 2.0 convert_bitcast_fusion.3
  174.1 4.1 copy.42
  178.2 0.0 copy-done.3
  178.2 2.4 copy.43
  180.6 4.9 fusion.37
  185.4 3.3 copy.44
  188.8 0.7 convert_bitcast_fusion
  189.5 0.9 copy-done.5
  190.4 0.6 copy-done.6
  191.0 5.7 pad_maximum_fusion
  196.7 9.6 %copy.45 = bf16[4,16,256,256]{3,2,0,1:T(8,128)(2,1)} copy(bf16[4,16,256,256]{3,1,2,0:T(8,128)(2,1)} %pad_maximum_fusion) | data formatting | bytes 16777216 | tf_op jit(solution)/shard_map/stack | solution.py:27
  206.3 0.0 all-to-all-done
  206.3 5.6 all-to-all-start.1
  212.0 0.6 fusion.63
  212.6 0.1 all_to_all.43
  212.7 2.8 gather_fusion
  215.5 2.8 gather_fusion.1
  218.3 2.5 compare_select_fusion.9
  220.8 0.1 iota_compare_fusion.1
  220.9 85.0 %all-to-all-done.1 = bf16[4,16,256,256]{3,2,0,1:T(8,128)(2,1)} async-done(((bf16[4,16,256,256]{3,2,0,1:T(8,128)(2,1)}), bf16[4,16,256,256]{3,2,0,1:T(8,128)(2,1)}, u32[]{:S(2)}, u32[]{:S(2)}) %all-to-all-start.1) | async-done | bytes 8388640 | tf_op jit(solution)/shard_map/all_to_all | solution.py:30
  305.9 7.8 %copy.46 = bf16[4,8,2,256,256]{4,3,0,1,2:T(8,128)(2,1)} copy(bf16[4,8,2,256,256]{4,3,0,2,1:T(8,128)(2,1)} %bitcast.44) | data formatting | bytes 16777216 | tf_op jit(solution)/shard_map/all_to_all | solution.py:30
  313.6 5.8 fusion
  319.4 1.5 copy-done.7
  321.0 3.3 fusion.1
  324.2 6.2 %pad_maximum_fusion.1 = bf16[32,2,256,256]{3,2,0,1:T(8,128)(2,1)} fusion(bf16[32,1,256,256]{3,2,0,1:T(8,128)(2,1)} %fusion.1, bf16[32,1,256,256]{3,2,0,1:T(8,128)(2,1)S(1)} %copy-done.9), kind=kLoop, calls=%fused_computation.11 | loop fusion | flops 4194304 | bytes 16777216 | tf_op jit(solution)/shard_map/stack | solution.py:42
  330.4 7.6 %copy.47 = bf16[32,2,256,256]{3,2,1,0:T(8,128)(2,1)} copy(bf16[32,2,256,256]{3,2,0,1:T(8,128)(2,1)} %pad_maximum_fusion.1) | data formatting | bytes 16777216 | tf_op jit(solution)/shard_map/stack | solution.py:42
  338.0 101.5 %all_to_all.55 = bf16[32,2,256,256]{3,2,1,0:T(8,128)(2,1)} all-to-all(bf16[32,2,256,256]{3,2,1,0:T(8,128)(2,1)} %copy.47), channel_id=1, replica_groups=mesh['row'=8,'col'=16] {'row'}, dimensions={0} | all-to-all | bytes 16777216 | tf_op jit(solution)/shard_map/all_to_all | solution.py:42
  439.5 7.6 %copy.48 = bf16[4,8,2,256,256]{4,3,2,1,0:T(8,128)(2,1)} copy(bf16[4,8,2,256,256]{4,3,2,0,1:T(8,128)(2,1)} %bitcast.153) | data formatting | bytes 16777216 | tf_op jit(solution)/shard_map/all_to_all | solution.py:42
  447.1 0.0 all-reduce.3.cloned.1.call-update
  447.2 0.6 copy-done.14
  447.8 0.6 dynamic-slice
  448.4 138.3 %all-reduce.3.cloned.1.call-done = bf16[4,16,256,256]{3,2,1,0:T(8,128)(2,1)} async-done(((bf16[4,16,256,256]{3,2,1,0:T(8,128)(2,1)}), bf16[4,16,256,256]{3,2,1,0:T(8,128)(2,1)}) %all-reduce.3.cloned.1.call-update) | async-done | bytes 8388624
  586.7 2.7 select_convert_fusion.2
  (35 shorter events, 0.1 us)
Async XLA Ops:
  6.5 206.2 %copy-start = (bf16[1,4,256,256]{3,2,1,0:T(8,128)(2,1)S(1)}, bf16[1,4,256,256]{3,2,1,0:T(8,128)(2,1)}, u32[]{:S(2)}) copy-start(bf16[1,4,256,256]{3,2,1,0:T(8,128)(2,1)} %param.12) | copy-start | bytes 1572868
  6.5 77.1 %all-gather.3.cloned.1.call-start = ((), (), s32[]{:S(2)}) async-start(), calls=%async_computation.3 | async-start | bytes 8912896 | tf_op jit(solution)/shard_map/all_gather | solution.py:11
  26.3 180.1 %all-to-all-start = ((s32[4,8,2]{0,2,1:T(2,128)}), s32[4,8,2]{0,2,1:T(2,128)S(1)}, u32[]{:S(2)}, u32[]{:S(2)}) async-start(s32[4,8,2]{0,2,1:T(2,128)} %bitcast.3), calls=%async_computation | async-start | bytes 16384 | tf_op jit(solution)/shard_map/all_to_all | solution.py:31
  124.4 4.1 copy-start.10
  148.8 4.6 copy-start.11
  153.4 2.1 copy-start.1
  155.5 6.0 copy-start.4
  174.1 4.1 copy-start.3
  188.8 1.6 copy-start.5
  188.8 2.2 copy-start.6
  206.3 5.6 copy-start.12
  206.3 99.5 %all-to-all-start.1 = ((bf16[4,16,256,256]{3,2,0,1:T(8,128)(2,1)}), bf16[4,16,256,256]{3,2,0,1:T(8,128)(2,1)}, u32[]{:S(2)}, u32[]{:S(2)}) async-start(bf16[4,16,256,256]{3,2,0,1:T(8,128)(2,1)} %copy.45), calls=%async_computation.1 | async-start | bytes 16777216 | tf_op jit(solution)/shard_map/all_to_all | solution.py:30
  212.0 374.7 %all-reduce.3.cloned.1.call-start = ((), (), s32[]{:S(2)}) async-start(), calls=%async_computation.4 | async-start | bytes 16777216
  305.8 7.8 %copy-start.8 = (bf16[32,256,256]{2,1,0:T(8,128)(2,1)S(1)}, bf16[32,256,256]{2,1,0:T(8,128)(2,1)}, u32[]{:S(2)}) copy-start(bf16[32,256,256]{2,1,0:T(8,128)(2,1)} %gather_fusion) | copy-start | bytes 12582916
  313.6 5.8 copy-start.2
  313.6 7.3 %copy-start.7 = (bf16[32,256,256]{2,1,0:T(8,128)(2,1)S(1)}, bf16[32,256,256]{2,1,0:T(8,128)(2,1)}, u32[]{:S(2)}) copy-start(bf16[32,256,256]{2,1,0:T(8,128)(2,1)} %gather_fusion.1) | copy-start | bytes 12582916
  321.0 3.3 copy-start.9
  447.1 0.7 copy-start.14
  447.1 139.6 %copy-start.13 = (s32[4]{0:T(128)S(1)}, s32[4]{0:T(128)}, u32[]{:S(2)}) copy-start(s32[4]{0:T(128)} %param.14) | copy-start | bytes 52
Sparse Core Ops, SparseCore 0:
  9.5 74.1 all-gather.2
  447.3 139.3 all-reduce.2
where the time goes:
time: 598 us; the launch traced here: 596 us
  waiting for transfers between devices  271 us (45%)
  local copies, waits for them, and re-layouts  125 us (21%)
  blocking collectives  120 us (20%)
  matrix products  34.7 us (6%)
  other arithmetic  17.2 us (3%)
  starting transfers between devices  15.2 us (3%)
  between operations  13.6 us (2%)
    unnamed x3, waiting for transfers between devices  139 us
    all_to_all x1, blocking collectives, per_device(): lax.all_to_all(jnp.stack(pieces, axis=1), 'row', split_axis=0, concat_axi...  101 us
    all_to_all x1, waiting for transfers between devices, per_device(): lax.all_to_all(mixed, 'row', split_axis=1, concat_axis=0, tiled=True)  85 us
    gather x17, local copies, waits for them, and re-layouts, per_device(): blocks = whole[left_src[0, position]]  65.5 us
    all_gather x1, waiting for transfers between devices, per_device(): lax.all_gather(wavefunction, 'col', axis=1, tiled=True)  46.7 us
    dot_general x4, matrix products, per_device(): jnp.einsum('kxy,ksyz->sxz', env_left[0, position], blocks, preferred_elem...  18.8 us
    all_gather x1, blocking collectives, per_device(): lax.all_gather(right_loc, 'col', axis=1, tiled=True)  18.3 us
    convert_element_type x4, local copies, waits for them, and re-layouts, per_device(): left_part = jnp.einsum('kxy,ksyz->sxz', env_left[0, position], blocks, pr...  14.6 us
  transfers between devices with their start and end apart: 4, of which 3 were waited for; matrix products, arithmetic and copies ran while one was open for 22% of the time, Pallas kernels for 0%

commit v1 on v0

--- a/solution.py
+++ b/solution.py
@@ -8,7 +8,9 @@
     wavefunction, env_left, left_src, two_site, env_right, right_loc, left_size, right_size
 ):
     whole, whole_loc = (
-        lax.all_gather(wavefunction, "col", axis=1, tiled=True),
+        jnp.concatenate(
+            lax.all_to_all(jnp.stack([wavefunction] * lax.axis_size("col")), "col", 0, 0), axis=1
+        ),
         lax.all_gather(right_loc, "col", axis=1, tiled=True),
     )
     local_tiles = wavefunction.shape[0]

time: 598 us -> 683 us (1.14)
  blocking collectives: 120 us -> 233 us
  waiting for transfers between devices: 271 us -> 222 us
  local copies, waits for them, and re-layouts: 125 us -> 137 us
  starting transfers between devices: 15.2 us -> 23 us
    all_gather x1, blocking collectives: 18.3 us -> 132 us  [per_device(): lax.all_gather(right_loc, 'col', axis=1, tiled=True)]
    all_gather x1 -> x0, waiting for transfers between devices: 46.7 us -> none  [per_device(): lax.all_gather(wavefunction, 'col', axis=1, tiled=True)]
    all_to_all x0 -> x1, starting transfers between devices: none -> 8.61 us  [per_device(): lax.all_to_all(jnp.stack([wavefunction] * lax.axis_size('col')), 'col', 0...]
    all_to_all x0 -> x1, local copies, waits for them, and re-layouts: none -> 7.61 us  [per_device(): lax.all_to_all(jnp.stack([wavefunction] * lax.axis_size('col')), 'col', 0...]
    unnamed x3 -> x2, waiting for transfers between devices: 139 us -> 137 us
  transfers between devices with their start and end apart: 4 -> 4, of which waited for: 3 -> 2; matrix products, arithmetic and copies ran while one was open for 22% -> 20% of each run, Pallas kernels for 0% -> 0%
where the time goes in v1:
time: 683 us; the launch traced here: 682 us
  blocking collectives  233 us (34%)
  waiting for transfers between devices  222 us (33%)
  local copies, waits for them, and re-layouts  137 us (20%)
  matrix products  34.7 us (5%)
  starting transfers between devices  23 us (3%)
  other arithmetic  17.3 us (3%)
  between operations  13.6 us (2%)
    unnamed x2, waiting for transfers between devices  137 us
    all_gather x1, blocking collectives, per_device(): lax.all_gather(right_loc, 'col', axis=1, tiled=True)  132 us
    all_to_all x1, blocking collectives, per_device(): lax.all_to_all(jnp.stack(pieces, axis=1), 'row', split_axis=0, concat_axi...  101 us
    all_to_all x1, waiting for transfers between devices, per_device(): lax.all_to_all(mixed, 'row', split_axis=1, concat_axis=0, tiled=True)  84.8 us
    gather x17, local copies, waits for them, and re-layouts, per_device(): blocks = whole[left_src[0, position]]  65.6 us
    dot_general x4, matrix products, per_device(): jnp.einsum('kxy,ksyz->sxz', env_left[0, position], blocks, preferred_elem...  18.8 us
    convert_element_type x4, local copies, waits for them, and re-layouts, per_device(): left_part = jnp.einsum('kxy,ksyz->sxz', env_left[0, position], blocks, pr...  14.6 us
  transfers between devices with their start and end apart: 4, of which 2 were waited for; matrix products, arithmetic and copies ran while one was open for 20% of the time, Pallas kernels for 0%

profile of v1, /device:TPU:1, one launch (start us, length us, event | category | flops | bytes accessed | tf_op | source)
XLA Modules:
  0.0 681.5 jit_solution(164634971758297709)
XLA Ops:
  6.5 5.4 stack.18
  11.9 8.6 %all-to-all-start.1 = ((bf16[16,4,1,256,256]{4,3,1,2,0:T(8,128)(2,1)}), bf16[16,4,1,256,256]{4,3,1,2,0:T(8,128)(2,1)}, u32[]{:S(2)}, u32[]{:S(2)}) async-start(bf16[16,4,1,256,256]{4,3,1,2,0:T(8,128)(2,1)} %stack.18), calls=%async_computation.1 | async-start | bytes 16777216 | tf_op jit(solution)/shard_map/all_to_all | solution.py:12
  20.5 131.8 %all-gather = s32[16,1,4]{2,1,0:T(1,128)S(1)} all-gather(s32[1,1,4]{2,1,0:T(1,128)S(1)} %bitcast.166), channel_id=1, replica_groups=mesh['row'=8,'col'=16] {'col'}, dimensions={0}, use_global_device_ids=true | all-gather | bytes 272 | tf_op jit(solution)/shard_map/all_gather | solution.py:14
  152.4 0.1 copy.49
  152.4 0.7 copy.50
  153.1 0.2 slice_reduce_fusion.3
  153.4 0.0 all-to-all-done.1
  153.4 9.3 %all-to-all-start = ((s32[4,8,2]{0,2,1:T(2,128)}), s32[4,8,2]{0,2,1:T(2,128)S(1)}, u32[]{:S(2)}, u32[]{:S(2)}) async-start(s32[4,8,2]{0,2,1:T(2,128)} %bitcast.3), calls=%async_computation | async-start | bytes 16384 | tf_op jit(solution)/shard_map/all_to_all | solution.py:33
  162.7 7.6 %copy.76 = bf16[16,4,1,256,256]{4,3,0,1,2:T(8,128)(2,1)} copy(bf16[16,4,1,256,256]{4,3,1,2,0:T(8,128)(2,1)} %all-to-all-done.1) | data formatting | bytes 16777216 | tf_op jit(solution)/shard_map/all_to_all | solution.py:12
  170.3 6.0 fusion.62
  176.3 2.9 gather_fusion.4
  179.1 4.2 gather_fusion.5
  183.4 4.2 gather_fusion.2
  187.5 4.2 gather_fusion.3
  191.8 4.2 gather_fusion.6
  196.0 4.2 gather_fusion.7
  200.2 4.2 gather_fusion.8
  204.4 4.2 gather_fusion.9
  208.6 2.4 copy.56
  211.0 4.1 copy.57
  215.1 4.2 fusion.31
  219.3 3.3 copy.58
  222.6 4.0 copy.53
  226.6 4.0 copy.54
  230.6 4.9 fusion.28
  235.4 4.6 copy.55
  240.1 2.1 convert_bitcast_fusion.2
  242.1 2.0 convert_bitcast_fusion.3
  244.1 4.0 copy.59
  248.1 2.4 copy.60
  250.5 4.9 fusion.34
  255.4 3.3 copy.61
  258.7 2.0 convert_bitcast_fusion.1
  260.8 4.1 copy.62
  264.9 2.4 copy.63
  267.3 4.9 fusion.37
  272.1 3.3 copy.64
  275.5 0.7 convert_bitcast_fusion
  276.2 0.9 copy-done.5
  277.1 0.6 copy-done.6
  277.7 5.7 pad_maximum_fusion
  283.4 9.6 %copy.65 = bf16[4,16,256,256]{3,2,0,1:T(8,128)(2,1)} copy(bf16[4,16,256,256]{3,1,2,0:T(8,128)(2,1)} %pad_maximum_fusion) | data formatting | bytes 16777216 | tf_op jit(solution)/shard_map/stack | solution.py:29
  293.0 5.0 all-to-all-start.2
  298.0 0.0 all-reduce.3.cloned.1.call-start
  298.1 0.7 fusion.63
  298.8 0.1 all_to_all.46
  298.9 2.8 gather_fusion
  301.7 2.8 gather_fusion.1
  304.4 2.5 compare_select_fusion.9
  307.0 0.1 iota_compare_fusion.1
  307.0 84.8 %all-to-all-done.2 = bf16[4,16,256,256]{3,2,0,1:T(8,128)(2,1)} async-done(((bf16[4,16,256,256]{3,2,0,1:T(8,128)(2,1)}), bf16[4,16,256,256]{3,2,0,1:T(8,128)(2,1)}, u32[]{:S(2)}, u32[]{:S(2)}) %all-to-all-start.2) | async-done | bytes 8388640 | tf_op jit(solution)/shard_map/all_to_all | solution.py:32
  391.8 7.8 %copy.66 = bf16[4,8,2,256,256]{4,3,0,1,2:T(8,128)(2,1)} copy(bf16[4,8,2,256,256]{4,3,0,2,1:T(8,128)(2,1)} %bitcast.48) | data formatting | bytes 16777216 | tf_op jit(solution)/shard_map/all_to_all | solution.py:32
  399.6 5.8 fusion
  405.4 1.5 copy-done.7
  407.0 3.3 fusion.1
  410.2 6.2 pad_maximum_fusion.1
  416.4 7.6 %copy.67 = bf16[32,2,256,256]{3,2,1,0:T(8,128)(2,1)} copy(bf16[32,2,256,256]{3,2,0,1:T(8,128)(2,1)} %pad_maximum_fusion.1) | data formatting | bytes 16777216 | tf_op jit(solution)/shard_map/stack | solution.py:44
  424.0 101.5 %all_to_all.60 = bf16[32,2,256,256]{3,2,1,0:T(8,128)(2,1)} all-to-all(bf16[32,2,256,256]{3,2,1,0:T(8,128)(2,1)} %copy.67), channel_id=1, replica_groups=mesh['row'=8,'col'=16] {'row'}, dimensions={0} | all-to-all | bytes 16777216 | tf_op jit(solution)/shard_map/all_to_all | solution.py:44
  525.5 7.6 %copy.68 = bf16[4,8,2,256,256]{4,3,2,1,0:T(8,128)(2,1)} copy(bf16[4,8,2,256,256]{4,3,2,0,1:T(8,128)(2,1)} %bitcast.160) | data formatting | bytes 16777216 | tf_op jit(solution)/shard_map/all_to_all | solution.py:44
  533.1 0.0 all-reduce.3.cloned.1.call-update
  533.1 0.6 copy-done.16
  533.8 0.7 dynamic-slice
  534.4 137.5 %all-reduce.3.cloned.1.call-done = bf16[4,16,256,256]{3,2,1,0:T(8,128)(2,1)} async-done(((bf16[4,16,256,256]{3,2,1,0:T(8,128)(2,1)}), bf16[4,16,256,256]{3,2,1,0:T(8,128)(2,1)}) %all-reduce.3.cloned.1.call-update) | async-done | bytes 8388624
  671.9 2.8 select_convert_fusion.2
  (40 shorter events, 0.1 us)
Async XLA Ops:
  6.5 292.3 %copy-start = (bf16[1,4,256,256]{3,2,1,0:T(8,128)(2,1)S(1)}, bf16[1,4,256,256]{3,2,1,0:T(8,128)(2,1)}, u32[]{:S(2)}) copy-start(bf16[1,4,256,256]{3,2,1,0:T(8,128)(2,1)} %param.12) | copy-start | bytes 1572868
  11.9 8.6 %copy-start.15 = (s32[4,1]{0,1:T(1,128)S(1)}, s32[4,1]{0,1:T(1,128)}, u32[]{:S(2)}) copy-start(s32[4,1]{0,1:T(1,128)} %param.13) | copy-start | bytes 52
  11.9 141.2 %copy-start.12 = (s32[1,4,2]{1,2,0:T(2,128)S(1)}, s32[1,4,2]{1,2,0:T(2,128)}, u32[]{:S(2)}) copy-start(s32[1,4,2]{1,2,0:T(2,128)} %param.10) | copy-start | bytes 100
  11.9 141.5 %all-to-all-start.1 = ((bf16[16,4,1,256,256]{4,3,1,2,0:T(8,128)(2,1)}), bf16[16,4,1,256,256]{4,3,1,2,0:T(8,128)(2,1)}, u32[]{:S(2)}, u32[]{:S(2)}) async-start(bf16[16,4,1,256,256]{4,3,1,2,0:T(8,128)(2,1)} %stack.18), calls=%async_computation.1 | async-start | bytes 16777216 | tf_op jit(solution)/shard_map/all_to_all | solution.py:12
  153.4 139.6 %all-to-all-start = ((s32[4,8,2]{0,2,1:T(2,128)}), s32[4,8,2]{0,2,1:T(2,128)S(1)}, u32[]{:S(2)}, u32[]{:S(2)}) async-start(s32[4,8,2]{0,2,1:T(2,128)} %bitcast.3), calls=%async_computation | async-start | bytes 16384 | tf_op jit(solution)/shard_map/all_to_all | solution.py:33
  211.0 4.1 copy-start.10
  235.4 4.6 copy-start.11
  240.0 2.1 copy-start.1
  242.1 6.0 copy-start.4
  260.8 4.1 copy-start.3
  275.5 1.6 copy-start.5
  275.5 2.2 copy-start.6
  293.0 5.1 copy-start.13
  293.0 98.9 %all-to-all-start.2 = ((bf16[4,16,256,256]{3,2,0,1:T(8,128)(2,1)}), bf16[4,16,256,256]{3,2,0,1:T(8,128)(2,1)}, u32[]{:S(2)}, u32[]{:S(2)}) async-start(bf16[4,16,256,256]{3,2,0,1:T(8,128)(2,1)} %copy.65), calls=%async_computation.2 | async-start | bytes 16777216 | tf_op jit(solution)/shard_map/all_to_all | solution.py:32
  298.0 373.8 %all-reduce.3.cloned.1.call-start = ((), (), s32[]{:S(2)}) async-start(), calls=%async_computation.4 | async-start | bytes 16777216
  391.8 7.8 %copy-start.8 = (bf16[32,256,256]{2,1,0:T(8,128)(2,1)S(1)}, bf16[32,256,256]{2,1,0:T(8,128)(2,1)}, u32[]{:S(2)}) copy-start(bf16[32,256,256]{2,1,0:T(8,128)(2,1)} %gather_fusion) | copy-start | bytes 12582916
  399.6 5.8 copy-start.2
  399.6 7.3 %copy-start.7 = (bf16[32,256,256]{2,1,0:T(8,128)(2,1)S(1)}, bf16[32,256,256]{2,1,0:T(8,128)(2,1)}, u32[]{:S(2)}) copy-start(bf16[32,256,256]{2,1,0:T(8,128)(2,1)} %gather_fusion.1) | copy-start | bytes 12582916
  407.0 3.3 copy-start.9
  533.1 0.7 copy-start.16
  533.1 138.8 %copy-start.14 = (s32[4]{0:T(128)S(1)}, s32[4]{0:T(128)}, u32[]{:S(2)}) copy-start(s32[4]{0:T(128)} %param.14) | copy-start | bytes 52
Sparse Core Ops, SparseCore 0:
  533.3 138.5 all-reduce.2
